TPU v7x, 256 devices: a whole 4x4x8 slice. The times are simulated.
256 devices in a mesh: seq: 32 (over z, y), exp: 8 (over x, core).
Axes of the slice: x: 4, y: 4, z: 8, core: 2. Of those that a mesh axis runs over, the one named last changes fastest.
Arguments:
- resid_rows: bfloat16 [8, 128, 3072], P('exp', 'seq'), may hold values from -6 to 6
- query_rows: bfloat16 [8, 128, 3072], P('exp', 'seq'), may hold values from -6 to 6
- key_rows: bfloat16 [8, 4096, 3072], P('exp', 'seq'), may hold values from -6 to 6
- value_rows: bfloat16 [8, 4096, 3072], P('exp', 'seq'), may hold values from -6 to 6
- log_decay: float32 [8, 48, 4096], P('exp', None, 'seq'), may hold values from -1 to 0
- read_pos: int32 [8, 128], P('exp', 'seq'), may hold values from 0 to 4095, as said below
- expert_ids: int32 [8, 128, 2], P('exp', 'seq'), may hold values from 0 to 7, all different within a row; in each aligned block of 4 rows (0 to 3, 4 to 7, ..., all dimensions but the last counted through in order) at most 2 rows name the same one
- pair_order: int32 [8], replicated, may hold values from 0 to 7, each once
- lengths: int32 [8], replicated, may hold values from 1 to 4096
- norm_gain: bfloat16 [3072], replicated, may hold values from 0.5 to 1.5
- router_weight: bfloat16 [3072, 8], replicated, may hold values from -0.109375 to 0.109375
- score_weight: bfloat16 [3072], replicated, may hold values from -0.109375 to 0.109375
- gate_weight: bfloat16 [8, 3072, 9216], P('exp', None, 'seq'), may hold values from -0.109375 to 0.109375
- up_weight: bfloat16 [8, 3072, 9216], P('exp', None, 'seq'), may hold values from -0.109375 to 0.109375
- down_weight: bfloat16 [8, 9216, 3072], P('exp', 'seq'), may hold values from -0.0625 to 0.0625
Outputs:
- pair_loss: float32 [], replicated
- grad_query: float32 [8, 128, 3072], P('exp', 'seq')
- grad_resid: float32 [8, 128, 3072], P('exp', 'seq')
- grad_keys: bfloat16 [8, 4096, 3072], P('exp', 'seq')
- grad_values: bfloat16 [8, 4096, 3072], P('exp', 'seq')
Inputs may be any that keep to these rules, and one draw needn't show every extreme that they name: `read_pos`: each aligned block j of 4 entries of a sequence holds strictly increasing positions from j * 128 to (j + 1) * 128 - 1, the last of them being (j + 1) * 128 - 1. `expert_ids`: the two entries of a row differ; in the rows of one device (aligned blocks of 4 rows) no expert is named by more than 2 rows. `pair_order`: each sequence appears once.
All inputs are finite; a program needn't handle non-finite values.
Results may differ from a plain program's by a relative error of at most 0.018.
Values may be sent and summed in bfloat16 or wider, within the bound.
No kernel may reach another device: no remote copies, remote signals or barrier semaphores. Data moves between devices by JAX's collectives and lax.ppermute only.
A program may use at most 128 MiB of HBM per device.

v0:
```python
import jax
import jax.numpy as jnp
from jax import lax
from jax.sharding import PartitionSpec as P

PRECISE = lax.Precision.HIGHEST
EPSILON = 1e-06
LENGTH_WEIGHT = 4.0
SCORE_SCALE = 256.0


def carried_in(value, axis, join, neutral, backward):
    count = lax.axis_size(axis)
    place = lax.axis_index(axis)
    ahead = count - 1 - place if backward else place
    gathered = jax.tree.map(
        lambda a, kind: lax.all_gather(a.astype(kind), axis), value, (jnp.bfloat16, jnp.bfloat16)
    )
    state = jax.tree.map(lambda a, e: jnp.zeros_like(a) + jnp.asarray(e, a.dtype), value, neutral)

    def one(lap, state):
        source = count - 1 - lap if backward else lap
        return join(
            state,
            jax.tree.map(
                lambda a, own: lax.dynamic_index_in_dim(a, source, 0, False).astype(own.dtype),
                gathered,
                value,
            ),
        )

    return lax.fori_loop(0, ahead, one, state)


def merge_states(earlier, later):
    return (earlier[0] * later[0], later[0][:, None, None] * earlier[1] + later[1])


def chain_prefix(decay, summary, backwards):
    blank = (jnp.ones_like(decay), jnp.zeros_like(summary))
    joined = carried_in((decay, summary), "seq", merge_states, blank, backwards)
    return joined[1]


def readout_weights(cumulated, places):
    positions = jnp.arange(cumulated.shape[1], dtype=jnp.int32)
    one_hot = (places[:, None] == positions[None, :]).astype(jnp.float32)
    at_read = jnp.dot(cumulated, one_hot.T, precision=PRECISE)
    allowed = positions[None, :] <= places[:, None]
    exponent = jnp.where(allowed[None], at_read[:, :, None] - cumulated[:, None, :], -1e30)
    return (at_read, jnp.exp(exponent))


def preference_loss(rewards, pair_order, lengths, total_length):
    count = rewards.shape[0]
    ordering = (pair_order[:, None] == jnp.arange(count, dtype=jnp.int32)[None, :]).astype(
        jnp.float32
    )
    ranked = jnp.dot(ordering, rewards, precision=PRECISE).reshape(count // 2, 2)
    fitted = jnp.mean(jax.nn.softplus(ranked[:, 1] - ranked[:, 0]))
    share = lengths.astype(jnp.float32) / total_length
    scatter_breadth = jnp.mean((rewards - jnp.mean(rewards)) * (share - jnp.mean(share)))
    return fitted + LENGTH_WEIGHT * scatter_breadth * scatter_breadth


def to_experts(slots):
    return lax.all_to_all(slots, "exp", split_axis=0, concat_axis=0, tiled=True)


def over_slots(arrived, project):
    return project(lax.all_gather(arrived, "seq", axis=0, tiled=True), jnp.int32(0))


def collect(project, expert_count, capacity):
    slot_count = expert_count * capacity
    summed = lax.psum_scatter(
        project(jnp.int32(0), slot_count * lax.axis_size("seq")).astype(jnp.bfloat16),
        "seq",
        scatter_dimension=0,
        tiled=True,
    )
    shaped = summed.reshape(expert_count, capacity, -1)
    return lax.all_to_all(shaped, "exp", split_axis=0, concat_axis=0, tiled=True)


def per_device(
    resid_rows,
    query_rows,
    key_rows,
    value_rows,
    log_decay,
    read_pos,
    expert_ids,
    pair_order,
    lengths,
    norm_gain,
    router_weight,
    score_weight,
    gate_weight,
    up_weight,
    down_weight,
):
    seq_count = lax.axis_size("seq")
    exp_count = lax.axis_size("exp")
    seq_index = lax.axis_index("seq")
    exp_index = lax.axis_index("exp")
    token_count = key_rows.shape[1]
    model_width = key_rows.shape[2]
    head_count = log_decay.shape[1]
    head_size = model_width // head_count
    read_count = query_rows.shape[1]
    expert_count = router_weight.shape[1]
    capacity = max(2, 4 * read_count // exp_count)
    keys_half = key_rows[0].reshape(token_count, head_count, head_size)
    values_half = value_rows[0].reshape(token_count, head_count, head_size)
    query_half = query_rows[0].reshape(read_count, head_count, head_size)
    keys_float = keys_half.astype(jnp.float32)
    values_float = values_half.astype(jnp.float32)
    query_float = query_half.astype(jnp.float32)
    cumulated = jnp.cumsum(log_decay[0], axis=1)
    group_decay = jnp.exp(cumulated[:, -1])
    tail_decay = jnp.exp(cumulated[:, -1:] - cumulated).T[:, :, None]
    own_state = jnp.einsum("thi,thj->hij", keys_float * tail_decay, values_float, precision=PRECISE)
    state_in = chain_prefix(group_decay, own_state, False)
    places = read_pos[0] - seq_index * token_count
    at_read, weight = readout_weights(cumulated, places)
    lift = jnp.exp(at_read).T[:, :, None]
    query_key = (
        jnp.einsum("rhi,thi->hrt", query_half, keys_half, preferred_element_type=jnp.float32)
        / head_size
    )
    attended = jnp.einsum("hrt,thj->rhj", weight * query_key, values_float, precision=PRECISE)
    attended = (
        attended
        + lift * jnp.einsum("rhi,hij->rhj", query_float, state_in, precision=PRECISE) / head_size
    )
    residual = resid_rows[0].astype(jnp.float32) + attended.reshape(read_count, model_width)
    inverse = lax.rsqrt(jnp.mean(residual * residual, axis=1, keepdims=True) + EPSILON)
    unit_rows = residual * inverse
    gain_float = norm_gain.astype(jnp.float32)
    normed = (unit_rows * gain_float).astype(jnp.bfloat16)
    logits = jnp.dot(normed, router_weight, preferred_element_type=jnp.float32)
    picks = (
        expert_ids[0][:, :, None] == jnp.arange(expert_count, dtype=jnp.int32)[None, None, :]
    ).astype(jnp.float32)
    chosen = jnp.einsum("rke,re->rk", picks, logits, precision=PRECISE)
    first = jax.nn.sigmoid(chosen[:, 0] - chosen[:, 1])
    gates = jnp.stack([first, 1.0 - first], axis=1)
    flat = picks.reshape(read_count * 2, expert_count)
    earlier = jnp.cumsum(flat, axis=0) - flat
    slot_index = jnp.sum(earlier * flat, axis=1)
    slot_hot = (slot_index[:, None] == jnp.arange(capacity, dtype=jnp.float32)[None, :]).astype(
        jnp.float32
    )
    placement = (
        (flat[:, :, None] * slot_hot[:, None, :])
        .reshape(read_count * 2, expert_count * capacity)
        .astype(jnp.bfloat16)
    )
    doubled = jnp.repeat(normed, 2, axis=0)
    outgoing = jnp.dot(placement.T, doubled, preferred_element_type=jnp.float32).astype(
        jnp.bfloat16
    )
    arrived = to_experts(outgoing.reshape(expert_count, capacity, model_width)).reshape(
        expert_count * capacity, model_width
    )
    gate_w = gate_weight[0]
    up_w = up_weight[0]
    down_w = down_weight[0]
    hidden_count = gate_w.shape[1]

    def project_in(piece, start):
        gate_part = jnp.dot(piece, gate_w, preferred_element_type=jnp.float32)
        up_part = jnp.dot(piece, up_w, preferred_element_type=jnp.float32)
        return jnp.concatenate([gate_part, up_part], axis=1)

    projected = over_slots(arrived, project_in)
    pre_gate = projected[:, :hidden_count]
    pre_up = projected[:, hidden_count:]
    gate_sigmoid = jax.nn.sigmoid(pre_gate)
    activated = (pre_gate * gate_sigmoid * pre_up).astype(jnp.bfloat16)

    def project_out(start, count):
        return jnp.dot(activated, down_w, preferred_element_type=jnp.float32)

    returned = collect(project_out, expert_count, capacity)
    expert_out = jnp.dot(
        placement,
        returned.reshape(expert_count * capacity, model_width),
        preferred_element_type=jnp.float32,
    )
    expert_out = expert_out.reshape(read_count, 2, model_width)
    mixed = residual + jnp.sum(gates[:, :, None] * expert_out, axis=1)
    score_float = score_weight.astype(jnp.float32)
    score = jnp.dot(mixed, score_float, precision=PRECISE)
    own_total = jnp.sum(score) / (read_count * seq_count)
    marked = jnp.where(jnp.arange(exp_count) == exp_index, own_total, 0.0)
    rewards = lax.psum(marked, ("seq", "exp"))
    pair_loss, d_reward = jax.value_and_grad(preference_loss)(
        rewards, pair_order, lengths, token_count * seq_count
    )
    own_grad = jnp.sum(jnp.where(jnp.arange(exp_count) == exp_index, d_reward, 0.0)) * SCORE_SCALE
    d_mixed = jnp.broadcast_to((own_grad * score_float)[None, :], (read_count, model_width))
    d_out = (gates[:, :, None] * d_mixed[:, None, :]).astype(jnp.bfloat16)
    d_gates = jnp.einsum("rd,rkd->rk", d_mixed, expert_out, precision=PRECISE)
    d_logit = (d_gates[:, 0] - d_gates[:, 1]) * first * (1.0 - first)
    back_out = jnp.dot(
        placement.T, d_out.reshape(read_count * 2, model_width), preferred_element_type=jnp.float32
    ).astype(jnp.bfloat16)
    back_arrived = to_experts(back_out.reshape(expert_count, capacity, model_width)).reshape(
        expert_count * capacity, model_width
    )

    def project_back(piece, start):
        return jnp.einsum("sd,fd->sf", piece, down_w, preferred_element_type=jnp.float32)

    d_act = over_slots(back_arrived, project_back)
    d_pre_gate = (d_act * pre_up * gate_sigmoid * (1.0 + pre_gate * (1.0 - gate_sigmoid))).astype(
        jnp.bfloat16
    )
    d_pre_up = (d_act * pre_gate * gate_sigmoid).astype(jnp.bfloat16)

    def project_in_back(start, count):
        gate_term = jnp.einsum("sf,df->sd", d_pre_gate, gate_w, preferred_element_type=jnp.float32)
        up_term = jnp.einsum("sf,df->sd", d_pre_up, up_w, preferred_element_type=jnp.float32)
        return gate_term + up_term

    d_in_slots = collect(project_in_back, expert_count, capacity)
    d_in = jnp.dot(
        placement,
        d_in_slots.reshape(expert_count * capacity, model_width),
        preferred_element_type=jnp.float32,
    )
    d_in = d_in.reshape(read_count, 2, model_width)
    columns = jnp.einsum("rke,de->rkd", picks, router_weight.astype(jnp.float32), precision=PRECISE)
    d_normed = jnp.sum(d_in, axis=1) + d_logit[:, None] * (columns[:, 0] - columns[:, 1])
    d_unit = d_normed * gain_float
    grad_resid = d_mixed + inverse * (
        d_unit - unit_rows * jnp.mean(d_unit * unit_rows, axis=1, keepdims=True)
    )
    rounded = grad_resid.astype(jnp.bfloat16)
    d_half = rounded.reshape(read_count, head_count, head_size)
    d_attended = d_half.astype(jnp.float32)
    summary = (
        jnp.einsum("rhi,rhj->hij", query_float * lift, d_attended, precision=PRECISE) / head_size
    )
    suffix = chain_prefix(group_decay, summary, True)
    grad_dot = (
        jnp.einsum("rhj,thj->hrt", d_half, values_half, preferred_element_type=jnp.float32)
        / head_size
    )
    grad_query = jnp.einsum("hrt,thi->rhi", weight * grad_dot, keys_float, precision=PRECISE)
    grad_query = (
        grad_query
        + lift * jnp.einsum("rhj,hij->rhi", d_attended, state_in, precision=PRECISE) / head_size
    )
    grad_keys = jnp.einsum("hrt,rhi->thi", weight * grad_dot, query_float, precision=PRECISE)
    grad_keys = grad_keys + tail_decay * jnp.einsum(
        "hij,thj->thi", suffix, values_float, precision=PRECISE
    )
    grad_values = jnp.einsum("hrt,rhj->thj", weight * query_key, d_attended, precision=PRECISE)
    grad_values = grad_values + tail_decay * jnp.einsum(
        "thi,hij->thj", keys_float, suffix, precision=PRECISE
    )
    return (
        pair_loss,
        grad_query.reshape(1, read_count, model_width),
        grad_resid.reshape(1, read_count, model_width),
        grad_keys.reshape(1, token_count, model_width).astype(jnp.bfloat16),
        grad_values.reshape(1, token_count, model_width).astype(jnp.bfloat16),
    )


def solution(mesh):
    in_specs = (
        P("exp", "seq", None),
        P("exp", "seq", None),
        P("exp", "seq", None),
        P("exp", "seq", None),
        P("exp", None, "seq"),
        P("exp", "seq"),
        P("exp", "seq", None),
        P(),
        P(),
        P(),
        P(),
        P(),
        P("exp", None, "seq"),
        P("exp", None, "seq"),
        P("exp", "seq", None),
    )
    out_specs = (
        P(),
        P("exp", "seq", None),
        P("exp", "seq", None),
        P("exp", "seq", None),
        P("exp", "seq", None),
    )
    return jax.shard_map(
        per_device, mesh=mesh, in_specs=in_specs, out_specs=out_specs, check_vma=False
    )
```

profile of v0, /device:TPU:1, one launch (start us, length us, event | category | flops | bytes accessed | tf_op | source)
XLA Modules:
  0.0 1303.2 jit_solution(8809889284805440682)
XLA Ops:
  8.7 1.5 copy.58
  10.2 1.8 copy.60
  12.1 2.2 fusion.17
  16.3 65.9 %all-reduce.2 = bf16[1536]{0:T(1024)(128)(2,1)S(1)} all-reduce(bf16[1536]{0:T(1024)(128)(2,1)S(1)} %dynamic-update-slice), channel_id=2, replica_groups=mesh['seq'=32,'exp'=8] {'seq'}, use_global_device_ids=true, to_apply=%add.2 | all-reduce | flops 1536 | bytes 6144
  87.4 2.0 convolution_bitcast_fusion.3
  89.4 111.9 %all-gather.12.cloned.1.call-done = bf16[1536,64,64]{2,1,0:T(8,128)(2,1)} async-done(((bf16[48,64,64]{2,1,0:T(8,128)(2,1)}), bf16[1536,64,64]{2,1,0:T(8,128)(2,1)}) %all-gather.12.cloned.1.call-update) | async-done | bytes 12582928 | tf_op jit(solution)/shard_map/all_gather | solution.py:17
  201.5 1.8 multiply_reduce_fusion.1
  204.4 1.6 reshape.388
  209.6 1.6 convolution_convert_fusion.2
  211.2 1.6 reshape.390
  212.8 10.7 all_to_all.20
  223.5 1.6 reshape.391
  225.1 137.3 %all-gather.8.cloned.1.call-done = bf16[512,3072]{1,0:T(8,128)(2,1)} async-done(((bf16[16,3072]{1,0:T(8,128)(2,1)}), bf16[512,3072]{1,0:T(8,128)(2,1)}) %all-gather.8.cloned.1.call-update) | async-done | bytes 3145744 | tf_op jit(solution)/shard_map/all_gather | solution.py:71
  362.4 3.7 fusion.8
  368.3 3.5 convolution_convert_fusion
  382.1 207.1 %reduce-scatter.3.cloned.1.call-done = bf16[16,3072]{1,0:T(8,128)(2,1)} async-done(((bf16[512,3072]{1,0:T(8,128)(2,1)}), bf16[16,3072]{1,0:T(8,128)(2,1)}) %reduce-scatter.3.cloned.1.call-update) | async-done | bytes 98320 | tf_op jit(solution)/shard_map/reduce_scatter | solution.py:76
  589.2 1.6 reshape.392
  590.8 10.0 all-to-all-start.1
  603.3 2.6 all-to-all-done.1
  605.9 1.6 reshape.419
  607.4 1.7 multiply_reduce_fusion
  609.1 1.7 fusion.32
  613.3 74.1 %psum.7 = f32[8]{0:T(128)} all-reduce(f32[8]{0:T(128)} %compare_select_fusion.4), channel_id=1, replica_groups=mesh['seq'=32,'exp'=8] {'seq','exp'}, use_global_device_ids=true, to_apply=%region_9.10 | all-reduce | flops 8 | bytes 64 | tf_op jit(solution)/shard_map/psum | solution.py:198
  696.0 1.5 fusion.85
  702.9 1.5 convolution_convert_fusion.1
  704.4 1.6 reshape.396
  705.9 9.6 all_to_all.21
  715.5 1.6 reshape.397
  717.2 72.2 %all-gather.10.cloned.1.call-done = bf16[512,3072]{1,0:T(8,128)(2,1)} async-done(((bf16[16,3072]{1,0:T(8,128)(2,1)}), bf16[512,3072]{1,0:T(8,128)(2,1)}) %all-gather.10.cloned.1.call-update) | async-done | bytes 3145744 | tf_op jit(solution)/shard_map/all_gather | solution.py:71
  789.4 3.1 fusion
  792.6 2.0 fusion.6
  794.7 3.7 add_convert_fusion
  800.2 215.3 %reduce-scatter.5.cloned.1.call-done = bf16[16,3072]{1,0:T(8,128)(2,1)} async-done(((bf16[512,3072]{1,0:T(8,128)(2,1)}), bf16[16,3072]{1,0:T(8,128)(2,1)}) %reduce-scatter.5.cloned.1.call-update) | async-done | bytes 98320 | tf_op jit(solution)/shard_map/reduce_scatter | solution.py:76
  1015.6 1.6 reshape.398
  1017.2 10.0 all-to-all-start.3
  1027.3 4.9 all-to-all-done.3
  1033.6 3.2 multiply_convert_fusion
  1044.5 2.0 fusion.62
  1046.5 2.0 fusion.88
  1049.3 167.0 %all-gather.14.cloned.1.call-done = bf16[1536,64,64]{2,1,0:T(8,128)(2,1)} async-done(((bf16[48,64,64]{2,1,0:T(8,128)(2,1)}), bf16[1536,64,64]{2,1,0:T(8,128)(2,1)}) %all-gather.14.cloned.1.call-update) | async-done | bytes 12582928 | tf_op jit(solution)/shard_map/all_gather | solution.py:17
  1216.5 68.8 %while.27 = (s32[]{:T(128)}, f32[48,64,64]{2,1,0:T(8,128)S(1)}, s32[]{:T(128)}, bf16[32,48]{1,0:T(8,128)(2,1)}, bf16[32,48,64,64]{3,2,1,0:T(8,128)(2,1)}, /*index=5*/s32[]{:T(128)}, s32[]{:T(128)}, s32[]{:T(128)}, s32[]{:T(128)}) while((s32[]{:T(128)}, f32[48,64,64]{2,1,0:T(8,128)S(1)}, s32[]{:T(128)}, bf16[32,48]{1,0:T(8,128)(2,1)}, ...), condition=%wide.region_20.21_spmd, body=%wide.region_19.20_spmd.sunk | while | flops 589878 | bytes 1966715 | solution.py:32
  1217.2 1.5 convert_add_fusion.5
  1219.4 1.5 convert_add_fusion.5
  1245.9 1.5 convert_add_fusion.5
  1261.4 1.5 convert_add_fusion.5
  1285.3 2.4 fusion.13
  1288.9 4.1 fusion.11
  1293.0 2.3 copy.78
  (254 shorter events, 112.9 us)
Async XLA Ops:
  7.2 361.1 %copy-start = (bf16[1,288,3072]{2,1,0:T(8,128)(2,1)S(1)}, bf16[1,288,3072]{2,1,0:T(8,128)(2,1)}, u32[]{:S(2)}) copy-start(bf16[1,288,3072]{2,1,0:T(8,128)(2,1)} %param.33) | copy-start | bytes 5308420
  7.2 194.1 %all-gather.12.cloned.1.call-start = ((), (), s32[]{:S(2)}) async-start(), calls=%async_computation.10 | async-start | bytes 25952256 | tf_op jit(solution)/shard_map/all_gather | solution.py:17
  8.4 77.3 %copy-start.24 = (f32[48,128]{1,0:T(8,128)}, f32[48,128]{1,0:T(8,128)S(1)}, u32[]{:S(2)}) copy-start(f32[48,128]{1,0:T(8,128)S(1)} %reduce_window_sum.22) | copy-start | bytes 73732
  8.7 3.3 copy-start.21
  10.2 75.5 %copy-start.2 = (bf16[1,128,3072]{1,2,0:T(8,128)(2,1)}, bf16[1,128,3072]{1,2,0:T(8,128)(2,1)S(1)}, u32[]{:S(2)}) copy-start(bf16[1,128,3072]{1,2,0:T(8,128)(2,1)S(1)} %copy.58) | copy-start | bytes 2359300
  12.0 74.8 %copy-start.4 = (bf16[1,128,3072]{1,2,0:T(8,128)(2,1)}, bf16[1,128,3072]{1,2,0:T(8,128)(2,1)S(1)}, u32[]{:S(2)}) copy-start(bf16[1,128,3072]{1,2,0:T(8,128)(2,1)S(1)} %copy.60) | copy-start | bytes 2359300
  12.0 2.4 copy-start.40
  12.0 2.6 copy-start.37
  12.0 2.6 copy-start.50
  12.0 70.9 %copy-start.49 = (s32[1,4]{1,0:T(1,128)S(1)}, s32[1,4]{1,0:T(1,128)}, u32[]{:S(2)}) copy-start(s32[1,4]{1,0:T(1,128)} %param.24) | copy-start | bytes 52
  12.1 72.5 %copy-start.36 = (bf16[1,4,3072]{2,1,0:T(4,128)(2,1)S(1)}, bf16[1,4,3072]{2,1,0:T(4,128)(2,1)}, u32[]{:S(2)}) copy-start(bf16[1,4,3072]{2,1,0:T(4,128)(2,1)} %param.20) | copy-start | bytes 73732
  12.1 72.6 %copy-start.25 = (bf16[1,4,3072]{2,1,0:T(4,128)(2,1)S(1)}, bf16[1,4,3072]{2,1,0:T(4,128)(2,1)}, u32[]{:S(2)}) copy-start(bf16[1,4,3072]{2,1,0:T(4,128)(2,1)} %param.19) | copy-start | bytes 73732
  14.3 348.1 %all-gather.8.cloned.1.call-start = ((), (), s32[]{:S(2)}) async-start(), calls=%async_computation.6 | async-start | bytes 3244032 | tf_op jit(solution)/shard_map/all_gather | solution.py:71
  84.6 116.8 %copy-start.12 = (bf16[4,48,64]{2,1,0:T(8,128)(2,1)}, bf16[4,48,64]{2,1,0:T(8,128)(2,1)S(1)}, u32[]{:S(2)}) copy-start(bf16[4,48,64]{2,1,0:T(8,128)(2,1)S(1)} %reshape_squeeze.9) | copy-start | bytes 73732
  85.7 115.8 %copy-start.52 = (pred[4,128]{1,0:T(4,128)(4,1)}, pred[4,128]{1,0:T(4,128)(4,1)S(1)}, u32[]{:S(2)}) copy-start(pred[4,128]{1,0:T(4,128)(4,1)S(1)} %iota_compare_fusion.6) | copy-start | bytes 1540
  225.1 364.1 %reduce-scatter.3.cloned.1.call-start = ((), (), s32[]{:S(2)}) async-start(), calls=%async_computation.7 | async-start | bytes 3244032 | tf_op jit(solution)/shard_map/reduce_scatter | solution.py:76
  362.4 3.7 copy-start.9
  362.4 3.9 copy-start.48
  366.3 1.1 copy-start.6
  590.8 15.1 %all-to-all-start.1 = ((bf16[8,2,3072]{2,1,0:T(2,128)(2,1)}), bf16[8,2,3072]{2,1,0:T(2,128)(2,1)}, u32[]{:S(2)}, u32[]{:S(2)}) async-start(bf16[8,2,3072]{2,1,0:T(2,128)(2,1)} %reshape.392), calls=%async_computation.2 | async-start | bytes 196608 | tf_op jit(solution)/shard_map/all_to_all | solution.py:83
  600.8 188.6 %all-gather.10.cloned.1.call-start = ((), (), s32[]{:S(2)}) async-start(), calls=%async_computation.8 | async-start | bytes 3244032 | tf_op jit(solution)/shard_map/all_gather | solution.py:71
  717.1 298.5 %reduce-scatter.5.cloned.1.call-start = ((), (), s32[]{:S(2)}) async-start(), calls=%async_computation.9 | async-start | bytes 3244032 | tf_op jit(solution)/shard_map/reduce_scatter | solution.py:76
  789.4 3.2 copy-start.7
  789.4 3.2 copy-start.8
  789.4 3.2 copy-start.17
  792.6 2.0 copy-start.10
  798.3 228.8 %copy-start.45 = (f32[4,1]{0,1:T(1,128)S(1)}, f32[4,1]{0,1:T(1,128)}, u32[]{:S(2)}) copy-start(f32[4,1]{0,1:T(1,128)} %get-tuple-element.175) | copy-start | bytes 52
  798.4 233.9 %copy-start.39 = (bf16[4,2,16]{2,0,1:T(4,128)(2,1)S(1)}, bf16[4,2,16]{2,0,1:T(4,128)(2,1)}, u32[]{:S(2)}) copy-start(bf16[4,2,16]{2,0,1:T(4,128)(2,1)} %copy.67) | copy-start | bytes 772
  798.4 234.1 %copy-start.18 = (f32[4,3072]{1,0:T(4,128)S(1)}, f32[4,3072]{1,0:T(4,128)}, u32[]{:S(2)}) copy-start(f32[4,3072]{1,0:T(4,128)} %reshape.388) | copy-start | bytes 147460
  798.4 234.1 %copy-start.26 = (bf16[1,4,3072]{2,1,0:T(4,128)(2,1)S(1)}, bf16[1,4,3072]{2,1,0:T(4,128)(2,1)}, u32[]{:S(2)}) copy-start(bf16[1,4,3072]{2,1,0:T(4,128)(2,1)} %param.19) | copy-start | bytes 73732
  798.4 234.1 %copy-start.42 = (f32[4]{0:T(128)S(1)}, f32[4]{0:T(128)}, u32[]{:S(2)}) copy-start(f32[4]{0:T(128)} %add_rsqrt_fusion) | copy-start | bytes 52
  799.0 234.5 %copy-start.13 = (bf16[4,48,64]{2,1,0:T(8,128)(2,1)S(1)}, bf16[4,48,64]{2,1,0:T(8,128)(2,1)}, u32[]{:S(2)}) copy-start(bf16[4,48,64]{2,1,0:T(8,128)(2,1)} %copy-done.12) | copy-start | bytes 73732
  1017.2 15.0 %all-to-all-start.3 = ((bf16[8,2,3072]{2,1,0:T(2,128)(2,1)}), bf16[8,2,3072]{2,1,0:T(2,128)(2,1)S(1)}, u32[]{:S(2)}, u32[]{:S(2)}) async-start(bf16[8,2,3072]{2,1,0:T(2,128)(2,1)} %reshape.398), calls=%async_computation.5 | async-start | bytes 196608 | tf_op jit(solution)/shard_map/all_to_all | solution.py:83
  1027.2 189.1 %all-gather.14.cloned.1.call-start = ((), (), s32[]{:S(2)}) async-start(), calls=%async_computation.11 | async-start | bytes 25952256 | tf_op jit(solution)/shard_map/all_gather | solution.py:17
  1027.2 5.9 copy-start.43
  1027.3 9.5 copy-start.11
  1032.2 7.7 copy-start.5
  1033.5 7.5 copy-start.3
  1036.7 5.6 copy-start.23
  1042.3 4.1 copy-start.29
  1044.4 4.1 copy-start.15
  1044.4 4.1 copy-start.20
  1044.4 4.1 copy-start.27
  1044.4 4.1 copy-start.32
  1044.4 4.1 copy-start.44
  1044.5 4.1 copy-start.47
  1216.5 68.8 %copy-start.22 = (f32[128,48]{0,1:T(8,128)S(1)}, f32[128,48]{0,1:T(8,128)}, u32[]{:S(2)}) copy-start(f32[128,48]{0,1:T(8,128)} %copy-done.21) | copy-start | bytes 73732
  1288.9 6.4 copy-start.1
  (13 other events, 9.8 us)
Sparse Core Ops, SparseCore 0:
  14.5 186.7 all-gather.11
  225.2 137.1 all-gather.7
  371.9 217.2 reduce-scatter.2
  717.3 72.1 all-gather.9
  798.5 216.9 reduce-scatter.4
  1036.9 179.3 all-gather.13
where the time goes:
time: 1310 us; the launch traced here: 1300 us
  waiting for transfers between devices  918 us (70%)
  blocking collectives  160 us (12%)
  other arithmetic  85.5 us (7%)
  matrix products  54 us (4%)
  local copies, waits for them, and re-layouts  41.1 us (3%)
  between operations  22.6 us (2%)
  starting transfers between devices  20.2 us (2%)
    reduce_scatter x2, waiting for transfers between devices, collect(): lax.psum_scatter(project(jnp.int32(0), slot_count * lax.axis_size('seq'))...  422 us
    all_gather x2, waiting for transfers between devices, carried_in(): lax.all_gather(a.astype(kind), axis)  279 us
    all_gather x2, waiting for transfers between devices, over_slots(): lax.all_gather(arrived, 'seq', axis=0, tiled=True)  210 us
    psum x1, blocking collectives, per_device(): rewards = lax.psum(marked, ('seq', 'exp'))  74.1 us
    unnamed x1, blocking collectives  65.9 us
    add x31, other arithmetic, merge_states(): later[0][:, None, None] * earlier[1] + later[1]  46.5 us
  transfers between devices with their start and end apart: 8, of which 8 were waited for; matrix products, arithmetic and copies ran while one was open for 2% of the time, Pallas kernels for 0%

commit v1 on v0

--- a/solution.py
+++ b/solution.py
@@ -195,7 +195,7 @@
     score = jnp.dot(mixed, score_float, precision=PRECISE)
     own_total = jnp.sum(score) / (read_count * seq_count)
     marked = jnp.where(jnp.arange(exp_count) == exp_index, own_total, 0.0)
-    rewards = lax.psum(marked, ("seq", "exp"))
+    rewards = lax.psum(lax.psum(marked, "exp"), "seq")
     pair_loss, d_reward = jax.value_and_grad(preference_loss)(
         rewards, pair_order, lengths, token_count * seq_count
     )

time: 1310 us -> 1320 us (level)
    all_to_all x2, blocking collectives: 20.3 us -> 34.5 us  [to_experts(): return lax.all_to_all(slots, 'exp', split_axis=0, concat_axis=0, tiled=True)]
    psum x1 -> x2, blocking collectives: 74.1 us -> 72.2 us  [per_device(): rewards = lax.psum(lax.psum(marked, 'exp'), 'seq')]
where the time goes in v1:
time: 1320 us
  waiting for transfers between devices  919 us (70%)
  blocking collectives  173 us (13%)
  other arithmetic  85.9 us (7%)
  matrix products  54.1 us (4%)
  local copies, waits for them, and re-layouts  41.5 us (3%)
  between operations  22.9 us (2%)
  starting transfers between devices  20.2 us (2%)
    reduce_scatter x2, waiting for transfers between devices, collect(): lax.psum_scatter(project(jnp.int32(0), slot_count * lax.axis_size('seq'))...  423 us
    all_gather x2, waiting for transfers between devices, carried_in(): lax.all_gather(a.astype(kind), axis)  279 us
    all_gather x2, waiting for transfers between devices, over_slots(): lax.all_gather(arrived, 'seq', axis=0, tiled=True)  209 us
    psum x2, blocking collectives, per_device(): rewards = lax.psum(lax.psum(marked, 'exp'), 'seq')  72.2 us
    unnamed x1, blocking collectives  65.9 us
    add x31, other arithmetic, merge_states(): later[0][:, None, None] * earlier[1] + later[1]  46.5 us
    all_to_all x2, blocking collectives, to_experts(): return lax.all_to_all(slots, 'exp', split_axis=0, concat_axis=0, tiled=True)  34.5 us
  transfers between devices with their start and end apart: 8, of which 8 were waited for; matrix products, arithmetic and copies ran while one was open for 2% of the time, Pallas kernels for 0%

profile of v1, /device:TPU:1, one launch (start us, length us, event | category | flops | bytes accessed | tf_op | source)
XLA Modules:
  0.0 1317.1 jit_solution(17880184684053869841)
XLA Ops:
  8.7 1.5 copy.58
  10.2 1.8 copy.60
  12.1 2.2 fusion.17
  16.3 65.9 %all-reduce.2 = bf16[1536]{0:T(1024)(128)(2,1)S(1)} all-reduce(bf16[1536]{0:T(1024)(128)(2,1)S(1)} %dynamic-update-slice), channel_id=2, replica_groups=mesh['seq'=32,'exp'=8] {'seq'}, use_global_device_ids=true, to_apply=%add.2 | all-reduce | flops 1536 | bytes 6144
  87.4 2.0 convolution_bitcast_fusion.3
  89.4 111.9 %all-gather.12.cloned.1.call-done = bf16[1536,64,64]{2,1,0:T(8,128)(2,1)} async-done(((bf16[48,64,64]{2,1,0:T(8,128)(2,1)}), bf16[1536,64,64]{2,1,0:T(8,128)(2,1)}) %all-gather.12.cloned.1.call-update) | async-done | bytes 12582928 | tf_op jit(solution)/shard_map/all_gather | solution.py:17
  201.5 1.8 multiply_reduce_fusion.1
  204.5 1.6 reshape.388
  209.7 1.6 convolution_convert_fusion.2
  211.3 1.6 reshape.390
  212.9 10.7 all_to_all.20
  223.6 1.6 reshape.391
  225.2 137.3 %all-gather.8.cloned.1.call-done = bf16[512,3072]{1,0:T(8,128)(2,1)} async-done(((bf16[16,3072]{1,0:T(8,128)(2,1)}), bf16[512,3072]{1,0:T(8,128)(2,1)}) %all-gather.8.cloned.1.call-update) | async-done | bytes 3145744 | tf_op jit(solution)/shard_map/all_gather | solution.py:71
  362.5 3.7 fusion.8
  368.4 3.6 convolution_convert_fusion
  382.5 207.0 %reduce-scatter.3.cloned.1.call-done = bf16[16,3072]{1,0:T(8,128)(2,1)} async-done(((bf16[512,3072]{1,0:T(8,128)(2,1)}), bf16[16,3072]{1,0:T(8,128)(2,1)}) %reduce-scatter.3.cloned.1.call-update) | async-done | bytes 98320 | tf_op jit(solution)/shard_map/reduce_scatter | solution.py:76
  589.6 1.6 reshape.392
  591.1 9.7 all-to-all-start.1
  602.1 3.8 all-to-all-done.1
  605.9 1.6 reshape.419
  607.4 1.7 multiply_reduce_fusion
  609.1 1.7 fusion.32
  613.3 13.2 %psum.14 = f32[8]{0:T(128)} all-reduce(f32[8]{0:T(128)} %compare_select_fusion.4), channel_id=1, replica_groups=mesh['seq'=32,'exp'=8] {'exp'}, use_global_device_ids=true, to_apply=%region_9.10 | all-reduce | flops 8 | bytes 64 | tf_op jit(solution)/shard_map/psum | solution.py:198
  627.8 59.0 %psum.15 = f32[8]{0:T(128)} all-reduce(f32[8]{0:T(128)} %psum.14), channel_id=1, replica_groups=mesh['seq'=32,'exp'=8] {'seq'}, use_global_device_ids=true, to_apply=%region_10.11 | all-reduce | flops 8 | bytes 64 | tf_op jit(solution)/shard_map/psum | solution.py:198
  695.8 1.6 fusion.85
  699.4 1.5 fusion.31
  702.9 1.5 convolution_convert_fusion.1
  704.4 1.6 reshape.396
  706.0 23.8 %all_to_all.21 = bf16[8,2,3072]{2,1,0:T(2,128)(2,1)} all-to-all(bf16[8,2,3072]{2,1,0:T(2,128)(2,1)} %reshape.396), channel_id=1, replica_groups=mesh['seq'=32,'exp'=8] {'exp'}, dimensions={0} | all-to-all | bytes 196608 | tf_op jit(solution)/shard_map/all_to_all | solution.py:67
  729.8 1.6 reshape.397
  731.6 71.3 %all-gather.10.cloned.1.call-done = bf16[512,3072]{1,0:T(8,128)(2,1)} async-done(((bf16[16,3072]{1,0:T(8,128)(2,1)}), bf16[512,3072]{1,0:T(8,128)(2,1)}) %all-gather.10.cloned.1.call-update) | async-done | bytes 3145744 | tf_op jit(solution)/shard_map/all_gather | solution.py:71
  802.9 3.1 fusion
  806.1 2.0 fusion.6
  808.2 3.7 add_convert_fusion
  813.8 215.6 %reduce-scatter.5.cloned.1.call-done = bf16[16,3072]{1,0:T(8,128)(2,1)} async-done(((bf16[512,3072]{1,0:T(8,128)(2,1)}), bf16[16,3072]{1,0:T(8,128)(2,1)}) %reduce-scatter.5.cloned.1.call-update) | async-done | bytes 98320 | tf_op jit(solution)/shard_map/reduce_scatter | solution.py:76
  1029.4 1.6 reshape.398
  1030.9 10.2 all-to-all-start.3
  1041.2 4.9 all-to-all-done.3
  1047.5 3.2 multiply_convert_fusion
  1058.5 2.0 fusion.62
  1060.5 2.0 fusion.88
  1063.3 166.8 %all-gather.14.cloned.1.call-done = bf16[1536,64,64]{2,1,0:T(8,128)(2,1)} async-done(((bf16[48,64,64]{2,1,0:T(8,128)(2,1)}), bf16[1536,64,64]{2,1,0:T(8,128)(2,1)}) %all-gather.14.cloned.1.call-update) | async-done | bytes 12582928 | tf_op jit(solution)/shard_map/all_gather | solution.py:17
  1230.3 68.8 %while.27 = (s32[]{:T(128)}, f32[48,64,64]{2,1,0:T(8,128)S(1)}, s32[]{:T(128)}, bf16[32,48]{1,0:T(8,128)(2,1)}, bf16[32,48,64,64]{3,2,1,0:T(8,128)(2,1)}, /*index=5*/s32[]{:T(128)}, s32[]{:T(128)}, s32[]{:T(128)}, s32[]{:T(128)}) while((s32[]{:T(128)}, f32[48,64,64]{2,1,0:T(8,128)S(1)}, s32[]{:T(128)}, bf16[32,48]{1,0:T(8,128)(2,1)}, ...), condition=%wide.region_21.22_spmd, body=%wide.region_20.21_spmd.sunk | while | flops 589878 | bytes 1966715 | solution.py:32
  1231.0 1.5 convert_add_fusion.5
  1284.2 1.5 convert_add_fusion.5
  1299.1 2.4 fusion.13
  1302.7 4.1 fusion.11
  1306.8 2.3 copy.78
  (255 shorter events, 115.4 us)
Async XLA Ops:
  7.2 361.2 %copy-start = (bf16[1,288,3072]{2,1,0:T(8,128)(2,1)S(1)}, bf16[1,288,3072]{2,1,0:T(8,128)(2,1)}, u32[]{:S(2)}) copy-start(bf16[1,288,3072]{2,1,0:T(8,128)(2,1)} %param.33) | copy-start | bytes 5308420
  7.2 194.1 %all-gather.12.cloned.1.call-start = ((), (), s32[]{:S(2)}) async-start(), calls=%async_computation.10 | async-start | bytes 25952256 | tf_op jit(solution)/shard_map/all_gather | solution.py:17
  8.4 77.3 %copy-start.24 = (f32[48,128]{1,0:T(8,128)}, f32[48,128]{1,0:T(8,128)S(1)}, u32[]{:S(2)}) copy-start(f32[48,128]{1,0:T(8,128)S(1)} %reduce_window_sum.22) | copy-start | bytes 73732
  8.7 3.3 copy-start.21
  10.2 75.5 %copy-start.2 = (bf16[1,128,3072]{1,2,0:T(8,128)(2,1)}, bf16[1,128,3072]{1,2,0:T(8,128)(2,1)S(1)}, u32[]{:S(2)}) copy-start(bf16[1,128,3072]{1,2,0:T(8,128)(2,1)S(1)} %copy.58) | copy-start | bytes 2359300
  12.0 74.8 %copy-start.4 = (bf16[1,128,3072]{1,2,0:T(8,128)(2,1)}, bf16[1,128,3072]{1,2,0:T(8,128)(2,1)S(1)}, u32[]{:S(2)}) copy-start(bf16[1,128,3072]{1,2,0:T(8,128)(2,1)S(1)} %copy.60) | copy-start | bytes 2359300
  12.0 2.4 copy-start.40
  12.0 2.6 copy-start.37
  12.0 2.6 copy-start.50
  12.0 70.9 %copy-start.49 = (s32[1,4]{1,0:T(1,128)S(1)}, s32[1,4]{1,0:T(1,128)}, u32[]{:S(2)}) copy-start(s32[1,4]{1,0:T(1,128)} %param.24) | copy-start | bytes 52
  12.1 72.5 %copy-start.36 = (bf16[1,4,3072]{2,1,0:T(4,128)(2,1)S(1)}, bf16[1,4,3072]{2,1,0:T(4,128)(2,1)}, u32[]{:S(2)}) copy-start(bf16[1,4,3072]{2,1,0:T(4,128)(2,1)} %param.20) | copy-start | bytes 73732
  12.1 72.6 %copy-start.25 = (bf16[1,4,3072]{2,1,0:T(4,128)(2,1)S(1)}, bf16[1,4,3072]{2,1,0:T(4,128)(2,1)}, u32[]{:S(2)}) copy-start(bf16[1,4,3072]{2,1,0:T(4,128)(2,1)} %param.19) | copy-start | bytes 73732
  14.3 348.2 %all-gather.8.cloned.1.call-start = ((), (), s32[]{:S(2)}) async-start(), calls=%async_computation.6 | async-start | bytes 3244032 | tf_op jit(solution)/shard_map/all_gather | solution.py:71
  84.7 116.8 %copy-start.12 = (bf16[4,48,64]{2,1,0:T(8,128)(2,1)}, bf16[4,48,64]{2,1,0:T(8,128)(2,1)S(1)}, u32[]{:S(2)}) copy-start(bf16[4,48,64]{2,1,0:T(8,128)(2,1)S(1)} %reshape_squeeze.9) | copy-start | bytes 73732
  85.7 115.8 %copy-start.52 = (pred[4,128]{1,0:T(4,128)(4,1)}, pred[4,128]{1,0:T(4,128)(4,1)S(1)}, u32[]{:S(2)}) copy-start(pred[4,128]{1,0:T(4,128)(4,1)S(1)} %iota_compare_fusion.6) | copy-start | bytes 1540
  225.2 364.4 %reduce-scatter.3.cloned.1.call-start = ((), (), s32[]{:S(2)}) async-start(), calls=%async_computation.7 | async-start | bytes 3244032 | tf_op jit(solution)/shard_map/reduce_scatter | solution.py:76
  362.5 3.7 copy-start.9
  362.5 3.9 copy-start.48
  366.4 1.1 copy-start.6
  591.1 14.7 %all-to-all-start.1 = ((bf16[8,2,3072]{2,1,0:T(2,128)(2,1)}), bf16[8,2,3072]{2,1,0:T(2,128)(2,1)}, u32[]{:S(2)}, u32[]{:S(2)}) async-start(bf16[8,2,3072]{2,1,0:T(2,128)(2,1)} %reshape.392), calls=%async_computation.2 | async-start | bytes 196608 | tf_op jit(solution)/shard_map/all_to_all | solution.py:83
  600.8 202.2 %all-gather.10.cloned.1.call-start = ((), (), s32[]{:S(2)}) async-start(), calls=%async_computation.8 | async-start | bytes 3244032 | tf_op jit(solution)/shard_map/all_gather | solution.py:71
  731.4 298.0 %reduce-scatter.5.cloned.1.call-start = ((), (), s32[]{:S(2)}) async-start(), calls=%async_computation.9 | async-start | bytes 3244032 | tf_op jit(solution)/shard_map/reduce_scatter | solution.py:76
  802.9 3.2 copy-start.7
  802.9 3.2 copy-start.8
  802.9 3.2 copy-start.17
  806.1 2.0 copy-start.10
  811.9 229.2 %copy-start.45 = (f32[4,1]{0,1:T(1,128)S(1)}, f32[4,1]{0,1:T(1,128)}, u32[]{:S(2)}) copy-start(f32[4,1]{0,1:T(1,128)} %get-tuple-element.175) | copy-start | bytes 52
  811.9 234.3 %copy-start.39 = (bf16[4,2,16]{2,0,1:T(4,128)(2,1)S(1)}, bf16[4,2,16]{2,0,1:T(4,128)(2,1)}, u32[]{:S(2)}) copy-start(bf16[4,2,16]{2,0,1:T(4,128)(2,1)} %copy.67) | copy-start | bytes 772
  811.9 234.5 %copy-start.18 = (f32[4,3072]{1,0:T(4,128)S(1)}, f32[4,3072]{1,0:T(4,128)}, u32[]{:S(2)}) copy-start(f32[4,3072]{1,0:T(4,128)} %reshape.388) | copy-start | bytes 147460
  811.9 234.5 %copy-start.26 = (bf16[1,4,3072]{2,1,0:T(4,128)(2,1)S(1)}, bf16[1,4,3072]{2,1,0:T(4,128)(2,1)}, u32[]{:S(2)}) copy-start(bf16[1,4,3072]{2,1,0:T(4,128)(2,1)} %param.19) | copy-start | bytes 73732
  811.9 234.5 %copy-start.42 = (f32[4]{0:T(128)S(1)}, f32[4]{0:T(128)}, u32[]{:S(2)}) copy-start(f32[4]{0:T(128)} %add_rsqrt_fusion) | copy-start | bytes 52
  812.5 234.9 %copy-start.13 = (bf16[4,48,64]{2,1,0:T(8,128)(2,1)S(1)}, bf16[4,48,64]{2,1,0:T(8,128)(2,1)}, u32[]{:S(2)}) copy-start(bf16[4,48,64]{2,1,0:T(8,128)(2,1)} %copy-done.12) | copy-start | bytes 73732
  1030.9 15.1 %all-to-all-start.3 = ((bf16[8,2,3072]{2,1,0:T(2,128)(2,1)}), bf16[8,2,3072]{2,1,0:T(2,128)(2,1)S(1)}, u32[]{:S(2)}, u32[]{:S(2)}) async-start(bf16[8,2,3072]{2,1,0:T(2,128)(2,1)} %reshape.398), calls=%async_computation.5 | async-start | bytes 196608 | tf_op jit(solution)/shard_map/all_to_all | solution.py:83
  1041.1 189.0 %all-gather.14.cloned.1.call-start = ((), (), s32[]{:S(2)}) async-start(), calls=%async_computation.11 | async-start | bytes 25952256 | tf_op jit(solution)/shard_map/all_gather | solution.py:17
  1041.1 5.9 copy-start.43
  1041.2 9.5 copy-start.11
  1046.1 7.8 copy-start.5
  1047.5 7.6 copy-start.3
  1050.7 5.7 copy-start.23
  1056.4 4.1 copy-start.29
  1058.5 4.0 copy-start.15
  1058.5 4.0 copy-start.20
  1058.5 4.0 copy-start.27
  1058.5 4.0 copy-start.32
  1058.5 4.0 copy-start.44
  1058.5 4.0 copy-start.47
  1230.3 68.9 %copy-start.22 = (f32[128,48]{0,1:T(8,128)S(1)}, f32[128,48]{0,1:T(8,128)}, u32[]{:S(2)}) copy-start(f32[128,48]{0,1:T(8,128)} %copy-done.21) | copy-start | bytes 73732
  1302.7 6.4 copy-start.1
  (13 other events, 9.8 us)
Sparse Core Ops, SparseCore 0:
  14.5 186.7 all-gather.11
  225.3 137.1 all-gather.7
  372.1 217.4 reduce-scatter.2
  731.5 71.4 all-gather.9
  812.1 217.2 reduce-scatter.4
  1050.8 179.2 all-gather.13
